TPU v7x, 256 devices: a whole 4x4x8 slice. The times are simulated.
256 devices in a mesh: seg: 4 (over x), sec: 32 (over z, y), rep: 2 (over core).
Axes of the slice: x: 4, y: 4, z: 8, core: 2. Of those that a mesh axis runs over, the one named last changes fastest.
Arguments:
- psi: float32 [4, 64, 256, 256], P('seg', 'sec'), may hold values from -6 to 6
- left_env: bfloat16 [4, 18, 64, 256, 256], P('seg', 'rep', 'sec'), may hold values from -0.375 to 0.375
- right_env: bfloat16 [4, 18, 64, 256, 256], P('seg', 'rep', 'sec'), may hold values from -0.375 to 0.375
- local_block: bfloat16 [4, 64, 256, 256], P('seg', 'sec'), may hold values from -0.375 to 0.375
- kept_left: int32 [4, 64], P('seg', 'sec'), may hold values from 64 to 256
- kept_right: int32 [4, 64], P('seg', 'sec'), may hold values from 64 to 256
- pattern: int32 [4, 18, 64], P('seg', 'rep', 'sec'), may hold values 0 or 1
- term_charge: int32 [18], replicated, may hold values from -2 to 2
Outputs:
- last_vector: float32 [4, 64, 256, 256], P('seg', 'sec')
- coefficients: float32 [4, 8], P('seg')
All inputs are finite; a program needn't handle non-finite values. No bound on the sum of `pattern` on one device may be relied on, other than what follows from the above.
Results may differ from a plain program's by a relative error of at most 0.012.
Values may be sent and summed in bfloat16 or wider, within the bound.
A program may use at most 64 MiB of HBM per device.

v0:
```python
import jax
import jax.numpy as jnp
from jax import lax
from jax.sharding import PartitionSpec as P

ITERS = 4


def extended_2(shard, sides, width):
    for axis, dim in sides:
        size, length = (lax.axis_size(axis), shard.shape[dim])
        up = [(i, (i + 1) % size) for i in range(size - 1)]
        down = [(j, i) for i, j in up]
        last = lax.slice_in_dim(shard, length - width, length, axis=dim)
        first = lax.slice_in_dim(shard, 0, width, axis=dim)
        before = lax.ppermute(last, axis, up)
        after = lax.ppermute(first, axis, down)
        shard = jnp.concatenate([before, shard, after], axis=dim)
    return shard


def from_behind(shard, axis, by):
    length = lax.axis_size(axis)
    return lax.ppermute(shard, axis, [(i, (i + by) % length) for i in range(length)])


def widen(vb):
    return extended_2(vb, (("sec", 0),), 2)


def shifted(extended, charges, first, number):
    index = first + 2 + lax.iota(jnp.int32, number)[None, :] + charges[:, None]
    return extended[index]


def term_action(moved, lefts, rights, pat):
    inner = jnp.einsum("wsij,wsjk->wsik", lefts, moved, preferred_element_type=jnp.float32)
    inner = (inner * pat[:, :, None, None]).astype(jnp.bfloat16)
    return jnp.einsum("wsik,wslk->sil", inner, rights, preferred_element_type=jnp.float32)


def local_action(vb, block):
    first = jnp.einsum("sij,sjk->sik", block, vb, preferred_element_type=jnp.float32)
    return first + jnp.einsum("sij,skj->sik", vb, block, preferred_element_type=jnp.float32)


def lanczos(start, apply_op, mean_of):
    vector = start / jnp.sqrt(mean_of(start * start) + 1e-06)
    prev = jnp.zeros_like(vector)
    beta_prev = jnp.float32(0.0)
    alphas = []
    betas = []
    for step in range(ITERS):
        image = apply_op(vector)
        alpha = mean_of(vector * image)
        image = image - alpha * vector - beta_prev * prev
        beta = jnp.sqrt(mean_of(image * image) + 1e-06)
        prev = vector
        vector = image / beta
        beta_prev = beta
        alphas.append(alpha)
        betas.append(beta)
    return (vector, jnp.stack(alphas + betas))


def on_device(psi, left_env, right_env, local_block, kept_left, kept_right, pattern, term_charge):
    lefts = from_behind(left_env, "seg", 1)[0]
    rights = from_behind(right_env, "seg", -1)[0]
    start = psi[0]
    block = local_block[0]
    width = start.shape[1]
    sectors = start.shape[0]
    terms_here = lefts.shape[0]
    states = lax.iota(jnp.int32, width)
    rows = (states[None, :] < kept_left[0][:, None]).astype(jnp.float32)
    cols = (states[None, :] < kept_right[0][:, None]).astype(jnp.float32)
    projector = rows[:, :, None] * cols[:, None, :]
    count = sectors * lax.axis_size("sec") * width * width
    local_charge = lax.dynamic_slice_in_dim(
        term_charge, lax.axis_index("rep") * terms_here, terms_here, 0
    )
    pat = pattern[0].astype(jnp.float32)

    def apply_whole(vector):
        vb = vector.astype(jnp.bfloat16)
        moved = shifted(widen(vb), local_charge, 0, sectors)
        total = lax.psum(term_action(moved, lefts, rights, pat).astype(jnp.bfloat16), "rep").astype(
            jnp.float32
        )
        return projector * (total + local_action(vb, block))

    def mean_whole(values):
        return lax.psum(jnp.sum(values), "sec") / count

    vector, coeffs = lanczos(projector * start, apply_whole, mean_whole)
    return (vector[None], coeffs[None])


def solution(mesh):
    placed = (
        P("seg", "sec", None, None),
        P("seg", "rep", "sec", None, None),
        P("seg", "rep", "sec", None, None),
        P("seg", "sec", None, None),
        P("seg", "sec"),
        P("seg", "sec"),
        P("seg", "rep", "sec"),
        P(),
    )
    return jax.shard_map(
        on_device,
        mesh=mesh,
        in_specs=placed,
        out_specs=(P("seg", "sec", None, None), P("seg", None)),
        check_vma=False,
    )
```

profile of v0, /device:TPU:8, one launch (start us, length us, event | category | flops | bytes accessed | tf_op | source)
XLA Modules:
  0.0 898.0 jit_solution(11741691733564219125)
XLA Ops:
  7.3 3.4 copy.19
  10.7 2.8 collective-permute-start.3
  14.3 74.4 %psum.91 = f32[]{:T(128)} all-reduce(f32[]{:T(128)} %multiply_reduce_fusion.8), channel_id=1, replica_groups=mesh['seg'=4,'sec'=32,'rep'=2] {'sec'}, use_global_device_ids=true, to_apply=%region_1.0 | all-reduce | flops 1 | bytes 8 | tf_op jit(solution)/shard_map/psum | solution.py:93
  89.6 3.2 collective-permute-start
  92.8 4.6 collective-permute-start.1
  103.7 5.2 fusion.104
  109.2 32.2 %all-reduce.5.cloned.1.call-done = bf16[2,256,256]{2,1,0:T(8,128)(2,1)} async-done(((bf16[2,256,256]{2,1,0:T(8,128)(2,1)}), bf16[2,256,256]{2,1,0:T(8,128)(2,1)}) %all-reduce.5.cloned.1.call-update) | async-done | bytes 262160 | tf_op jit(solution)/shard_map/psum | solution.py:87
  143.4 71.8 %psum.93 = f32[]{:T(128)} all-reduce(f32[]{:T(128)} %get-tuple-element.10), channel_id=1, replica_groups=mesh['seg'=4,'sec'=32,'rep'=2] {'sec'}, use_global_device_ids=true, to_apply=%region_4.0 | all-reduce | flops 1 | bytes 8 | tf_op jit(solution)/shard_map/psum | solution.py:93
  216.7 74.8 %psum.94 = f32[]{:T(128)} all-reduce(f32[]{:T(128)} %multiply_reduce_fusion.6), channel_id=1, replica_groups=mesh['seg'=4,'sec'=32,'rep'=2] {'sec'}, use_global_device_ids=true, to_apply=%region_6.0 | all-reduce | flops 1 | bytes 8 | tf_op jit(solution)/shard_map/psum | solution.py:93
  294.3 3.9 collective-permute-start.5
  305.0 5.2 fusion.113
  310.5 30.3 %all-reduce.7.cloned.1.call-done = bf16[2,256,256]{2,1,0:T(8,128)(2,1)} async-done(((bf16[2,256,256]{2,1,0:T(8,128)(2,1)}), bf16[2,256,256]{2,1,0:T(8,128)(2,1)}) %all-reduce.7.cloned.1.call-update) | async-done | bytes 262160 | tf_op jit(solution)/shard_map/psum | solution.py:87
  342.8 71.8 %psum.96 = f32[]{:T(128)} all-reduce(f32[]{:T(128)} %get-tuple-element.12), channel_id=1, replica_groups=mesh['seg'=4,'sec'=32,'rep'=2] {'sec'}, use_global_device_ids=true, to_apply=%region_9.0 | all-reduce | flops 1 | bytes 8 | tf_op jit(solution)/shard_map/psum | solution.py:93
  416.1 74.8 %psum.97 = f32[]{:T(128)} all-reduce(f32[]{:T(128)} %get-tuple-element.6), channel_id=1, replica_groups=mesh['seg'=4,'sec'=32,'rep'=2] {'sec'}, use_global_device_ids=true, to_apply=%region_11.0 | all-reduce | flops 1 | bytes 8 | tf_op jit(solution)/shard_map/psum | solution.py:93
  493.6 3.9 collective-permute-start.7
  504.3 5.2 fusion.122
  509.8 30.3 %all-reduce.9.cloned.1.call-done = bf16[2,256,256]{2,1,0:T(8,128)(2,1)} async-done(((bf16[2,256,256]{2,1,0:T(8,128)(2,1)}), bf16[2,256,256]{2,1,0:T(8,128)(2,1)}) %all-reduce.9.cloned.1.call-update) | async-done | bytes 262160 | tf_op jit(solution)/shard_map/psum | solution.py:87
  542.1 71.8 %psum.99 = f32[]{:T(128)} all-reduce(f32[]{:T(128)} %get-tuple-element.14), channel_id=1, replica_groups=mesh['seg'=4,'sec'=32,'rep'=2] {'sec'}, use_global_device_ids=true, to_apply=%region_14.0 | all-reduce | flops 1 | bytes 8 | tf_op jit(solution)/shard_map/psum | solution.py:93
  615.3 74.8 %psum.100 = f32[]{:T(128)} all-reduce(f32[]{:T(128)} %get-tuple-element.4), channel_id=1, replica_groups=mesh['seg'=4,'sec'=32,'rep'=2] {'sec'}, use_global_device_ids=true, to_apply=%region_16.0 | all-reduce | flops 1 | bytes 8 | tf_op jit(solution)/shard_map/psum | solution.py:93
  692.8 4.1 collective-permute-start.9
  703.5 5.2 fusion.131
  709.0 30.4 %all-reduce.11.cloned.1.call-done = bf16[2,256,256]{2,1,0:T(8,128)(2,1)} async-done(((bf16[2,256,256]{2,1,0:T(8,128)(2,1)}), bf16[2,256,256]{2,1,0:T(8,128)(2,1)}) %all-reduce.11.cloned.1.call-update) | async-done | bytes 262160 | tf_op jit(solution)/shard_map/psum | solution.py:87
  741.3 71.8 %psum.102 = f32[]{:T(128)} all-reduce(f32[]{:T(128)} %get-tuple-element.16), channel_id=1, replica_groups=mesh['seg'=4,'sec'=32,'rep'=2] {'sec'}, use_global_device_ids=true, to_apply=%region_19.0 | all-reduce | flops 1 | bytes 8 | tf_op jit(solution)/shard_map/psum | solution.py:93
  814.6 74.8 %psum.103 = f32[]{:T(128)} all-reduce(f32[]{:T(128)} %get-tuple-element.2), channel_id=1, replica_groups=mesh['seg'=4,'sec'=32,'rep'=2] {'sec'}, use_global_device_ids=true, to_apply=%region_21.0 | all-reduce | flops 1 | bytes 8 | tf_op jit(solution)/shard_map/psum | solution.py:93
  (76 shorter events, 47.4 us)
Async XLA Ops:
  7.2 101.8 %copy-start = (bf16[1,2,256,256]{3,2,1,0:T(8,128)(2,1)S(1)}, bf16[1,2,256,256]{3,2,1,0:T(8,128)(2,1)}, u32[]{:S(2)}) copy-start(bf16[1,2,256,256]{3,2,1,0:T(8,128)(2,1)} %param.11) | copy-start | bytes 786436
  7.2 6.3 copy-start.8
  7.2 6.2 copy-start.7
  7.2 6.3 copy-start.1
  7.2 90.2 %copy-start.9 = (s32[18]{0:T(128)S(1)}, s32[18]{0:T(128)}, u32[]{:S(2)}) copy-start(s32[18]{0:T(128)} %param.15) | copy-start | bytes 220
  7.2 90.4 %copy-start.6 = (s32[1,9,2]{1,2,0:T(2,128)S(1)}, s32[1,9,2]{1,2,0:T(2,128)}, u32[]{:S(2)}) copy-start(s32[1,9,2]{1,2,0:T(2,128)} %param.14) | copy-start | bytes 220
  7.2 134.2 %all-reduce.5.cloned.1.call-start = ((), (), s32[]{:S(2)}) async-start(), calls=%async_computation | async-start | bytes 524288 | tf_op jit(solution)/shard_map/psum | solution.py:87
  10.7 93.0 %collective-permute-start.3 = (bf16[1,9,2,256,256]{4,3,1,2,0:T(8,128)(2,1)}, bf16[1,9,2,256,256]{4,3,1,2,0:T(8,128)(2,1)}, u32[]{:S(2)}, u32[]{:S(2)}) collective-permute-start(bf16[1,9,2,256,256]{4,3,1,2,0:T(8,128)(2,1)} %copy.19), channel_id=1, source_target_pairs={{0,192},{64,0},{128,64},{192,128},{1,193},{65,1},{129,65},{193,129... | collective-permute-start | bytes 7077896 | tf_op jit(solution)/shard_map/ppermute | solution.py:24
  13.4 90.3 %collective-permute-start.2 = (bf16[1,9,2,256,256]{4,3,2,1,0:T(8,128)(2,1)}, bf16[1,9,2,256,256]{4,3,2,1,0:T(8,128)(2,1)}, u32[]{:S(2)}, u32[]{:S(2)}) collective-permute-start(bf16[1,9,2,256,256]{4,3,2,1,0:T(8,128)(2,1)} %param.9), channel_id=1, source_target_pairs={{0,64},{64,128},{128,192},{192,0},{1,65},{65,129},{129,193},{193,1... | collective-permute-start | bytes 7077896 | tf_op jit(solution)/shard_map/ppermute | solution.py:24
  89.6 10.2 %collective-permute-start = (bf16[2,256,256]{2,1,0:T(8,128)(2,1)S(1)}, bf16[2,256,256]{2,1,0:T(8,128)(2,1)S(1)}, u32[]{:S(2)}, u32[]{:S(2)}) collective-permute-start(bf16[2,256,256]{2,1,0:T(8,128)(2,1)S(1)} %fusion.155), channel_id=1, source_target_pairs={{0,2},{2,4},{4,6},{6,8},{8,10},{10,12},{12,14},{14,16},{16,18},{18... | collective-permute-start | bytes 786440 | tf_op jit(solution)/shard_map/ppermute | solution.py:16
  92.8 8.5 collective-permute-start.1
  108.9 231.9 %all-reduce.7.cloned.1.call-start = ((), (), s32[]{:S(2)}) async-start(), calls=%async_computation.1 | async-start | bytes 524288 | tf_op jit(solution)/shard_map/psum | solution.py:87
  141.4 74.3 %copy-start.2 = (bf16[2,256,256]{2,1,0:T(8,128)(2,1)S(1)}, bf16[2,256,256]{2,1,0:T(8,128)(2,1)}, u32[]{:S(2)}) copy-start(bf16[2,256,256]{2,1,0:T(8,128)(2,1)} %all-reduce.5.cloned.1.call-done) | copy-start | bytes 786436
  292.4 8.3 collective-permute-start.4
  294.3 8.3 collective-permute-start.5
  310.2 229.9 %all-reduce.9.cloned.1.call-start = ((), (), s32[]{:S(2)}) async-start(), calls=%async_computation.2 | async-start | bytes 524288 | tf_op jit(solution)/shard_map/psum | solution.py:87
  340.9 74.3 %copy-start.3 = (bf16[2,256,256]{2,1,0:T(8,128)(2,1)S(1)}, bf16[2,256,256]{2,1,0:T(8,128)(2,1)}, u32[]{:S(2)}) copy-start(bf16[2,256,256]{2,1,0:T(8,128)(2,1)} %all-reduce.7.cloned.1.call-done) | copy-start | bytes 786436
  491.7 8.3 collective-permute-start.6
  493.6 8.3 collective-permute-start.7
  509.5 229.9 %all-reduce.11.cloned.1.call-start = ((), (), s32[]{:S(2)}) async-start(), calls=%async_computation.3 | async-start | bytes 524288 | tf_op jit(solution)/shard_map/psum | solution.py:87
  540.1 74.3 %copy-start.4 = (bf16[2,256,256]{2,1,0:T(8,128)(2,1)S(1)}, bf16[2,256,256]{2,1,0:T(8,128)(2,1)}, u32[]{:S(2)}) copy-start(bf16[2,256,256]{2,1,0:T(8,128)(2,1)} %all-reduce.9.cloned.1.call-done) | copy-start | bytes 786436
  690.9 8.3 collective-permute-start.8
  692.8 8.3 collective-permute-start.9
  739.4 74.3 %copy-start.5 = (bf16[2,256,256]{2,1,0:T(8,128)(2,1)S(1)}, bf16[2,256,256]{2,1,0:T(8,128)(2,1)}, u32[]{:S(2)}) copy-start(bf16[2,256,256]{2,1,0:T(8,128)(2,1)} %all-reduce.11.cloned.1.call-done) | copy-start | bytes 786436
Sparse Core Ops, SparseCore 0:
  109.0 32.3 all-reduce.4
  310.3 30.4 all-reduce.6
  509.6 30.4 all-reduce.8
  708.8 30.4 all-reduce.10
where the time goes:
time: 899 us; the launch traced here: 898 us
  blocking collectives  661 us (74%)
  waiting for transfers between devices  140 us (16%)
  matrix products  29.6 us (3%)
  starting transfers between devices  28.5 us (3%)
  between operations  20.1 us (2%)
  local copies, waits for them, and re-layouts  13.5 us (2%)
    psum x9, blocking collectives, mean_whole(): return lax.psum(jnp.sum(values), 'sec') / count  661 us
    psum x4, waiting for transfers between devices, apply_whole(): lax.psum(term_action(moved, lefts, rights, pat).astype(jnp.bfloat16), 'rep')  123 us
    dot_general x4, matrix products, term_action(): jnp.einsum('wsik,wslk->sil', inner, rights, preferred_element_type=jnp.fl...  20.8 us
  transfers between devices with their start and end apart: 14, of which 12 were waited for; matrix products, arithmetic and copies ran while one was open for 1% of the time, Pallas kernels for 0%

commit v1 on v0

v1 whole, which is shorter than its diff:
```python
import functools

import jax
import jax.numpy as jnp
from jax import lax
from jax.experimental import pallas as pl
from jax.experimental.pallas import tpu as pltpu
from jax.sharding import PartitionSpec as P

ITERS = 4
NY = 4
HALO = 2
F32 = jnp.float32
BF16 = jnp.bfloat16
MESH = pl.DeviceIdType.MESH


def nt_dot(a, b):
    return lax.dot_general(a, b, (((1,), (1,)), ((), ())), preferred_element_type=F32)


def column_sums(x):
    total = jnp.sum(x, axis=0, keepdims=True)
    width = total.shape[1] // 2
    return total[:, :width] + total[:, width:]


def kernel(
    nseg, nsec, here, size, count,
    psi, left, right, block, keep_l, keep_r, pattern, charge,
    out, coeffs,
    lbuf, rbuf, vs0, vs1, vs2, vs3, acc, mask, vs, us, ws, theirs,
    pat, index, red_z, red_y,
    l_send, r_send, l_recv, r_recv, halo_send, halo_recv,
    z_send, z_recv, y_send, y_recv, pat_send, pat_recv, fin_send, fin_recv,
):
    slots = (vs0, vs1, vs2, vs3)
    seg, sec, rep = lax.axis_index("seg"), lax.axis_index("sec"), lax.axis_index("rep")
    nz = nsec // NY
    z, y = sec // NY, sec % NY
    other = 1 - rep
    sector, sectors = 2 * sec + rep, 2 * nsec
    ahead, behind = (seg + 1) % nseg, (seg + nseg - 1) % nseg
    terms = 2 * here

    def at_sector(shift):
        s = (sector + sectors + shift) % sectors
        return (seg, s // 2, s % 2)

    shifts = (-1, 1, -2, 2)
    z_peers = [(seg, ((z + i) % nz) * NY + y, rep) for i in range(1, nz)]
    mine_y = 2 * y + rep
    y_peers = []
    for i in range(1, 2 * NY):
        p = (mine_y + i) % (2 * NY)
        y_peers.append((seg, z * NY + p // 2, p % 2))

    partners = [(a, sec, jnp.int32(r)) for a in (ahead, behind) for r in range(2)]
    partners += [at_sector(d) for d in shifts] + z_peers + y_peers
    barrier = pltpu.get_barrier_semaphore()
    for p in partners:
        pl.semaphore_signal(barrier, inc=1, device_id=p, device_id_type=MESH)
    pl.semaphore_wait(barrier, len(partners))

    def left_copy(t, r):
        w = rep * here + t
        return pltpu.make_async_remote_copy(
            left.at[0, t, r], lbuf.at[w], l_send, l_recv.at[w],
            device_id=(ahead, sec, jnp.int32(r)), device_id_type=MESH,
        )

    def right_copy(t, r):
        w = rep * here + t
        return pltpu.make_async_remote_copy(
            right.at[0, t, r], rbuf.at[w], r_send, r_recv.at[w],
            device_id=(behind, sec, jnp.int32(r)), device_id_type=MESH,
        )

    @pl.loop(0, here)
    def _(t):
        for r in range(2):
            left_copy(t, r).start()
            right_copy(t, r).start()

    def start_halo(k):
        for n, d in enumerate(shifts):
            pltpu.make_async_remote_copy(
                slots[k].at[HALO], slots[k].at[HALO - d],
                halo_send.at[k, n], halo_recv.at[k, n],
                device_id=at_sector(d), device_id_type=MESH,
            ).start()

    def wait_halo(k):
        for n, d in enumerate(shifts):
            pltpu.make_async_remote_copy(
                slots[k].at[HALO], slots[k].at[HALO - d],
                halo_send.at[k, n], halo_recv.at[k, n],
                device_id=at_sector(d), device_id_type=MESH,
            ).wait_recv()

    def exchange_start(buf, k, mine, peers, send, recv):
        for p in peers:
            pltpu.make_async_remote_copy(
                buf.at[k, mine], buf.at[k, mine], send.at[k], recv.at[k],
                device_id=p, device_id_type=MESH,
            ).start()

    def exchange_wait(buf, k, n, sem):
        some = buf.at[k, pl.ds(0, n)]
        pltpu.make_async_copy(some, some, sem.at[k]).wait()

    def total_of(buf, k, n):
        total = buf[k, 0]
        for i in range(1, n):
            total = total + buf[k, i]
        return total

    def reduce_first(k, rows):
        red_z[k, z] = jnp.zeros_like(red_z[k, 0])
        for i, row in enumerate(rows):
            red_z[k, z, pl.ds(i, 1), :] = row
        exchange_start(red_z, k, z, z_peers, z_send, z_recv)

    def reduce_second(k):
        exchange_wait(red_z, k, nz - 1, z_recv)
        red_y[k, mine_y] = total_of(red_z, k, nz)
        exchange_start(red_y, k, mine_y, y_peers, y_send, y_recv)

    def reduce_last(k):
        exchange_wait(red_y, k, 2 * NY - 1, y_recv)
        total = jnp.sum(total_of(red_y, k, 2 * NY), axis=1, keepdims=True)
        return total * (1.0 / count)

    rows = lax.broadcasted_iota(jnp.int32, (size, size), 0)
    cols = lax.broadcasted_iota(jnp.int32, (size, size), 1)
    inside = (rows < keep_l[0, rep]) & (cols < keep_r[0, rep])
    mask[...] = inside.astype(F32)
    start = mask[...] * psi[0, rep]
    vs[0] = start
    reduce_first(ITERS, [column_sums(start * start)])

    both = pattern[0].astype(F32)
    wide = (here, pat.shape[2])
    first, second = (jnp.broadcast_to(both[:, i : i + 1], wide) for i in range(2))
    zero = rep == 0
    pat[rep, pl.ds(0, here), :] = jnp.where(zero, first, second)
    pat[2, pl.ds(0, here), :] = jnp.where(zero, second, first)
    pat_copy = pltpu.make_async_remote_copy(
        pat.at[2], pat.at[rep], pat_send, pat_recv,
        device_id=(seg, sec, other), device_id_type=MESH,
    )
    pat_copy.start()
    pat_back = pltpu.make_async_remote_copy(
        pat.at[2], pat.at[other], pat_send, pat_recv,
        device_id=(seg, sec, other), device_id_type=MESH,
    )

    for k in range(ITERS):
        slots[k][2 * HALO + 1] = jnp.zeros((size, size), BF16)

    @pl.loop(0, terms)
    def _(w):
        c = charge[w]
        to = sector + c
        index[w] = jnp.where((to >= 0) & (to < sectors), c + HALO, 2 * HALO + 1)

    reduce_second(ITERS)
    scale = reduce_last(ITERS)[0:1]
    v0 = vs[0] * lax.rsqrt(scale + 1e-06)
    vs[0] = v0
    slots[0][HALO] = v0.astype(BF16)
    start_halo(0)
    pat_back.wait_recv()

    def local(k):
        own, blk = slots[k][HALO], block[0, rep]
        return jnp.dot(blk, own, preferred_element_type=F32) + nt_dot(own, blk)

    def term(k, q, t):
        w = q * here + t
        moved = slots[k][index[w]]
        inner = jnp.dot(lbuf[w], moved, preferred_element_type=F32)
        row = pat[q, pl.ds(t, 1), :]
        inner = (inner * jnp.concatenate([row, row], axis=1)).astype(BF16)
        return nt_dot(inner, rbuf[w])

    def env_wait(w):
        pltpu.make_async_remote_copy(
            left.at[0, 0, 0], lbuf.at[w], l_send, l_recv.at[w],
            device_id=(ahead, sec, rep), device_id_type=MESH,
        ).wait_recv()
        pltpu.make_async_remote_copy(
            right.at[0, 0, 0], rbuf.at[w], r_send, r_recv.at[w],
            device_id=(behind, sec, rep), device_id_type=MESH,
        ).wait_recv()

    acc[...] = local(0)
    wait_halo(0)

    @pl.loop(0, here)
    def _(t):
        env_wait(t)
        env_wait(here + t)
        acc[...] += term(0, 0, t) + term(0, 1, t)

    alphas, betas = [], []
    for k in range(ITERS):
        hv = mask[...] * acc[...]
        if k == 0:
            us[0] = hv
            ws[0] = hv
        else:
            means = reduce_last(k - 1)
            alpha = means[0:1]
            rest = means[1:2] - 2.0 * alpha * means[2:3] + alpha * alpha * means[3:4]
            beta = jnp.sqrt(jnp.maximum(rest, 0.0) + 1e-06)
            alphas.append(alpha)
            betas.append(beta)
            inverse = 1.0 / beta
            u = (hv - alpha * us[k - 1]) * inverse
            us[k] = u
            ws[k] = u - beta * vs[k - 1]
        if k < ITERS - 1:
            slots[k + 1][HALO] = ws[k].astype(BF16)
            start_halo(k + 1)
        if k > 0:
            vs[k] = (ws[k - 1] - alpha * vs[k - 1]) * inverse
        v, u, w = vs[k], us[k], ws[k]
        reduce_first(k, [column_sums(v * u), column_sums(w * w), column_sums(v * w), column_sums(v * v)])
        if k < ITERS - 1:
            acc[...] = local(k + 1)
            reduce_second(k)
            wait_halo(k + 1)

            @pl.loop(0, here)
            def _(t):
                acc[...] += term(k + 1, 0, t) + term(k + 1, 1, t)

    last = ITERS - 1

    def final_copy(i, buf):
        return pltpu.make_async_remote_copy(
            buf.at[last], theirs.at[i], fin_send.at[i], fin_recv.at[i],
            device_id=(seg, sec, other), device_id_type=MESH,
        )

    final_copy(0, ws).start()
    final_copy(1, vs).start()
    reduce_second(last)
    means = reduce_last(last)
    alpha = means[0:1]
    rest = means[1:2] - 2.0 * alpha * means[2:3] + alpha * alpha * means[3:4]
    beta = jnp.sqrt(jnp.maximum(rest, 0.0) + 1e-06)
    inverse = 1.0 / beta
    coeffs[...] = jnp.concatenate(alphas + [alpha] + betas + [beta], axis=1)
    out[0, rep] = (ws[last] - alpha * vs[last]) * inverse
    final_copy(0, ws).wait_recv()
    final_copy(1, vs).wait_recv()
    out[0, other] = (theirs[0] - alpha * theirs[1]) * inverse

    pltpu.make_async_copy(left, left, l_send).wait()
    pltpu.make_async_copy(right, right, r_send).wait()
    pat_copy.wait_send()
    final_copy(0, ws).wait_send()
    final_copy(1, vs).wait_send()
    for k in range(ITERS):
        for n, d in enumerate(shifts):
            pltpu.make_async_remote_copy(
                slots[k].at[HALO], slots[k].at[HALO - d],
                halo_send.at[k, n], halo_recv.at[k, n],
                device_id=at_sector(d), device_id_type=MESH,
            ).wait_send()
    for k in range(ITERS + 1):
        exchange_wait(red_z, k, nz - 1, z_send)
        exchange_wait(red_y, k, 2 * NY - 1, y_send)


def on_device(nseg, nsec, psi, left, right, block, keep_l, keep_r, pattern, charge):
    here, size = left.shape[1], left.shape[3]
    count = 2 * nsec * size * size
    nz = nsec // NY
    vmem = pl.BlockSpec(memory_space=pltpu.VMEM)
    smem = pl.BlockSpec(memory_space=pltpu.SMEM)
    anywhere = pl.BlockSpec(memory_space=pl.ANY)
    square = (size, size)
    dma = pltpu.SemaphoreType.DMA
    halo = pltpu.VMEM((2 * HALO + 2, *square), BF16)
    terms = 2 * here
    return pl.pallas_call(
        functools.partial(kernel, nseg, nsec, here, size, count),
        out_shape=(
            jax.ShapeDtypeStruct(psi.shape, F32),
            jax.ShapeDtypeStruct((1, 2 * ITERS), F32),
        ),
        in_specs=[vmem, anywhere, anywhere, vmem, smem, smem, vmem, smem],
        out_specs=(vmem, vmem),
        scratch_shapes=[
            pltpu.VMEM((terms, *square), BF16),
            pltpu.VMEM((terms, *square), BF16),
            halo, halo, halo, halo,
            pltpu.VMEM(square, F32),
            pltpu.VMEM(square, F32),
            pltpu.VMEM((ITERS, *square), F32),
            pltpu.VMEM((ITERS, *square), F32),
            pltpu.VMEM((ITERS, *square), F32),
            pltpu.VMEM((2, *square), F32),
            pltpu.VMEM((3, 16, 128), F32),
            pltpu.SMEM((terms,), jnp.int32),
            pltpu.VMEM((ITERS + 1, nz, 8, 128), F32),
            pltpu.VMEM((ITERS + 1, 2 * NY, 8, 128), F32),
            dma, dma, dma((terms,)), dma((terms,)),
            dma((ITERS, 4)), dma((ITERS, 4)),
            dma((ITERS + 1,)), dma((ITERS + 1,)),
            dma((ITERS + 1,)), dma((ITERS + 1,)),
            dma, dma, dma((2,)), dma((2,)),
        ],
        compiler_params=pltpu.CompilerParams(
            collective_id=0, has_side_effects=True, vmem_limit_bytes=48 << 20
        ),
    )(psi, left, right, block, keep_l, keep_r, pattern, charge)


def solution(mesh):
    placed = (
        P("seg", "sec", None, None),
        P("seg", "rep", "sec", None, None),
        P("seg", "rep", "sec", None, None),
        P("seg", "sec", None, None),
        P("seg", "sec"),
        P("seg", "sec"),
        P("seg", "rep", "sec"),
        P(),
    )
    return jax.shard_map(
        functools.partial(on_device, mesh.shape["seg"], mesh.shape["sec"]),
        mesh=mesh,
        in_specs=placed,
        out_specs=(P("seg", "sec", None, None), P("seg", None)),
        check_vma=False,
    )
```

time: 899 us -> 117 us (0.13)
  blocking collectives: 661 us -> 0 us
  waiting for transfers between devices: 140 us -> 0 us
  Pallas kernels: 0 us -> 105 us
  matrix products: 29.6 us -> 0 us
  starting transfers between devices: 28.5 us -> 0 us
  between operations: 20.1 us -> 0.65 us
    psum x9 -> x0, blocking collectives: 661 us -> none  [mean_whole(): return lax.psum(jnp.sum(values), 'sec') / count]
    psum x4 -> x0, waiting for transfers between devices: 123 us -> none  [apply_whole(): lax.psum(term_action(moved, lefts, rights, pat).astype(jnp.bfloat16), 'rep')]
    pallas_call x0 -> x1, Pallas kernels: none -> 105 us  [on_device(): pl.pallas_call(functools.partial(kernel, nseg, nsec, here, size, count),...]
    dot_general x12 -> x0, matrix products: 29.6 us -> none  [the longest x4 20.8 us: term_action(): jnp.einsum('wsik,wslk->sil', inner, rights, preferred_element_type=jnp.fl...]
    ppermute x10 -> x0, starting transfers between devices: 28.3 us -> none  [the longest x4 16.6 us: extended_2(): after = lax.ppermute(first, axis, down)]
    ppermute x10 -> x0, waiting for transfers between devices: 16.4 us -> none  [the longest x4 9.12 us: extended_2(): before = lax.ppermute(last, axis, up)]
    gather x4 -> x0, local copies, waits for them, and re-layouts: 9.3 us -> none  [shifted(): return extended[index]]
  transfers between devices with their start and end apart: 14 -> 0, of which waited for: 12 -> 0; matrix products, arithmetic and copies ran while one was open for 1% -> 0% of each run, Pallas kernels for 0% -> 0%
where the time goes in v1:
time: 117 us; the launch traced here: 115 us
  Pallas kernels  105 us (90%)
  local copies, waits for them, and re-layouts  9.36 us (8%)
    pallas_call x1, Pallas kernels, on_device(): pl.pallas_call(functools.partial(kernel, nseg, nsec, here, size, count),...  105 us
    unnamed x17, local copies, waits for them, and re-layouts  9.36 us

profile of v1, /device:TPU:8, one launch (start us, length us, event | category | flops | bytes accessed | tf_op | source)
XLA Modules:
  0.0 115.0 jit_solution(4993184716951249988)
XLA Ops:
  0.6 0.8 copy.10.pattern
  1.4 0.0 copy-start
  1.4 1.7 %copy-done = bf16[1,9,2,256,256]{4,3,2,1,0:T(8,128)(2,1)S(1)} copy-done((bf16[1,9,2,256,256]{4,3,2,1,0:T(8,128)(2,1)S(1)}, bf16[1,9,2,256,256]{4,3,2,1,0:T(8,128)(2,1)}, u32[]{:S(2)}) %copy-start) | copy-done | bytes 2359320
  3.1 0.0 copy-start.1
  3.1 1.7 %copy-done.1 = bf16[1,9,2,256,256]{4,3,2,1,0:T(8,128)(2,1)S(1)} copy-done((bf16[1,9,2,256,256]{4,3,2,1,0:T(8,128)(2,1)S(1)}, bf16[1,9,2,256,256]{4,3,2,1,0:T(8,128)(2,1)}, u32[]{:S(2)}) %copy-start.1) | copy-done | bytes 2359320
  4.7 0.0 copy-start.2
  4.7 1.0 copy-done.2
  5.8 0.0 copy-start.3
  5.8 0.9 copy-done.3
  6.7 0.0 copy-start.4
  6.7 0.7 copy-done.4
  7.4 0.0 copy-start.5
  7.4 0.7 copy-done.5
  8.0 0.0 copy-start.6
  8.0 0.7 copy-done.6
  8.7 105.0 %shard_map.95 = (f32[1,2,256,256]{3,2,1,0:T(8,128)S(1)}, f32[1,8]{1,0:T(1,128)S(1)}) custom-call(f32[1,2,256,256]{3,2,1,0:T(8,128)S(1)} %copy-done.2, bf16[1,9,2,256,256]{4,3,2,1,0:T(8,128)(2,1)S(1)} %copy-done, bf16[1,9,2,256,256]{4,3,2,1,0:T(8,128)(2,1)S(1)} %copy-done.1, bf16[1,2,256,256]{3,2,1,0:T(8,128)(2,1)S(1)} %copy-done.3, s32[1,2]{1,0:T(1,128)S(1)} %copy-done.4, ...), custom_call_target="tpu_custom_call" | custom-call | tf_op jit(solution)/shard_map/pallas_call | solution.py:289
  113.7 0.8 copy.13
  114.5 0.5 copy.14
Async XLA Ops:
  1.4 1.7 %copy-start = (bf16[1,9,2,256,256]{4,3,2,1,0:T(8,128)(2,1)S(1)}, bf16[1,9,2,256,256]{4,3,2,1,0:T(8,128)(2,1)}, u32[]{:S(2)}) copy-start(bf16[1,9,2,256,256]{4,3,2,1,0:T(8,128)(2,1)} %left.1) | copy-start | bytes 7077892
  3.1 1.7 %copy-start.1 = (bf16[1,9,2,256,256]{4,3,2,1,0:T(8,128)(2,1)S(1)}, bf16[1,9,2,256,256]{4,3,2,1,0:T(8,128)(2,1)}, u32[]{:S(2)}) copy-start(bf16[1,9,2,256,256]{4,3,2,1,0:T(8,128)(2,1)} %right.1) | copy-start | bytes 7077892
  4.7 1.0 copy-start.2
  5.8 0.9 copy-start.3
  6.7 0.7 copy-start.4
  7.4 0.7 copy-start.5
  8.0 0.7 copy-start.6

commit v2 on v1

v2 whole, which is shorter than its diff:
```python
import functools

import jax
import jax.numpy as jnp
from jax import lax
from jax.experimental import pallas as pl
from jax.experimental.pallas import tpu as pltpu
from jax.sharding import PartitionSpec as P

ITERS = 4
NY = 4
HALO = 2
ROUNDS = 4
INITIAL = ROUNDS - 1
SUMS = 16
F32 = jnp.float32
BF16 = jnp.bfloat16
MESH = pl.DeviceIdType.MESH


def nt_dot(a, b):
    return lax.dot_general(a, b, (((1,), (1,)), ((), ())), preferred_element_type=F32)


def outward(n):
    return sorted(range(1, n), key=lambda i: -min(i, n - i))


def column_sums(x):
    total = jnp.sum(x, axis=0, keepdims=True)
    width = total.shape[1] // 2
    return total[:, :width] + total[:, width:]


def kernel(
    nseg, nsec, here, size, count,
    psi, left, right, block, keep_l, keep_r, pattern, charge,
    out, coeffs,
    lbuf, rbuf, vs0, vs1, vs2, vs3, acc, mask, v0, e1, e2, v1, u1, w1, hu1, hw1, mine, theirs,
    psi_v, blk_v, pat_v, pat_s, kl_s, kr_s, charge_s, index, red_z, red_y,
    load, l_send, r_send, l_recv, r_recv, halo_send, halo_recv,
    z_send, z_recv, y_send, y_recv, pat_send, pat_recv, fin_send, fin_recv,
):
    slots = (vs0, vs1, vs2, vs3)
    seg, sec, rep = lax.axis_index("seg"), lax.axis_index("sec"), lax.axis_index("rep")
    nz = nsec // NY
    z, y = sec // NY, sec % NY
    other = 1 - rep
    sector, sectors = 2 * sec + rep, 2 * nsec
    ahead, behind = (seg + 1) % nseg, (seg + nseg - 1) % nseg
    terms = 2 * here

    def at_sector(shift):
        s = (sector + sectors + shift) % sectors
        return (seg, s // 2, s % 2)

    shifts = (-1, 1, -2, 2)
    z_peers = [(seg, ((z + i) % nz) * NY + y, rep) for i in outward(nz)]
    mine_y = 2 * y + rep
    y_peers = []
    for i in outward(2 * NY):
        p = (mine_y + i) % (2 * NY)
        y_peers.append((seg, z * NY + p // 2, p % 2))

    partners = [(a, sec, jnp.int32(r)) for a in (ahead, behind) for r in range(2)]
    partners += [at_sector(d) for d in shifts] + z_peers + y_peers
    barrier = pltpu.get_barrier_semaphore()
    for p in partners:
        pl.semaphore_signal(barrier, inc=1, device_id=p, device_id_type=MESH)
    loads = [
        pltpu.make_async_copy(a, b, load.at[i])
        for i, (a, b) in enumerate([
            (psi.at[0, rep], psi_v), (block.at[0, rep], blk_v), (pattern.at[0], pat_s.at[rep]),
            (keep_l, kl_s), (keep_r, kr_s), (charge, charge_s),
        ])
    ]
    for c in loads:
        c.start()
    pl.semaphore_wait(barrier, len(partners))

    def left_copy(t, r):
        w = rep * here + t
        return pltpu.make_async_remote_copy(
            left.at[0, t, r], lbuf.at[w], l_send, l_recv.at[w],
            device_id=(ahead, sec, jnp.int32(r)), device_id_type=MESH,
        )

    def right_copy(t, r):
        w = rep * here + t
        return pltpu.make_async_remote_copy(
            right.at[0, t, r], rbuf.at[w], r_send, r_recv.at[w],
            device_id=(behind, sec, jnp.int32(r)), device_id_type=MESH,
        )

    @pl.loop(0, here)
    def _(t):
        for r in range(2):
            left_copy(t, r).start()
            right_copy(t, r).start()

    def start_halo(k):
        for n, d in enumerate(shifts):
            pltpu.make_async_remote_copy(
                slots[k].at[HALO], slots[k].at[HALO - d],
                halo_send.at[k, n], halo_recv.at[k, n],
                device_id=at_sector(d), device_id_type=MESH,
            ).start()

    def wait_halo(k):
        for n, d in enumerate(shifts):
            pltpu.make_async_remote_copy(
                slots[k].at[HALO], slots[k].at[HALO - d],
                halo_send.at[k, n], halo_recv.at[k, n],
                device_id=at_sector(d), device_id_type=MESH,
            ).wait_recv()

    def exchange_start(buf, k, mine, peers, send, recv):
        for p in peers:
            pltpu.make_async_remote_copy(
                buf.at[k, mine], buf.at[k, mine], send.at[k], recv.at[k],
                device_id=p, device_id_type=MESH,
            ).start()

    def exchange_wait(buf, k, n, sem):
        some = buf.at[k, pl.ds(0, n)]
        pltpu.make_async_copy(some, some, sem.at[k]).wait()

    def total_of(buf, k, n):
        total = buf[k, 0]
        for i in range(1, n):
            total = total + buf[k, i]
        return total

    def reduce_first(k, rows):
        red_z[k, z] = jnp.zeros_like(red_z[k, 0])
        for i, row in enumerate(rows):
            red_z[k, z, pl.ds(i, 1), :] = row
        exchange_start(red_z, k, z, z_peers, z_send, z_recv)

    def reduce_second(k):
        exchange_wait(red_z, k, nz - 1, z_recv)
        red_y[k, mine_y] = total_of(red_z, k, nz)
        exchange_start(red_y, k, mine_y, y_peers, y_send, y_recv)

    def reduce_last(k):
        exchange_wait(red_y, k, 2 * NY - 1, y_recv)
        total = jnp.sum(total_of(red_y, k, 2 * NY), axis=1, keepdims=True)
        return total * (1.0 / count)

    pat_copy = pltpu.make_async_remote_copy(
        pattern.at[0], pat_v, pat_send, pat_recv, device_id=(seg, sec, other), device_id_type=MESH
    )
    pat_copy.start()
    for c in loads:
        c.wait()

    rows = lax.broadcasted_iota(jnp.int32, (size, size), 0)
    cols = lax.broadcasted_iota(jnp.int32, (size, size), 1)
    inside = (rows < kl_s[0, rep]) & (cols < kr_s[0, rep])
    mask[...] = inside.astype(F32)
    start = mask[...] * psi_v[...]
    v0[...] = start
    reduce_first(INITIAL, [column_sums(start * start)])

    pat_copy.wait_recv()
    move = pltpu.make_async_copy(pat_v, pat_s.at[other], load.at[0])
    move.start()
    move.wait()

    for k in range(ITERS):
        slots[k][2 * HALO + 1] = jnp.zeros((size, size), BF16)

    @pl.loop(0, terms)
    def _(w):
        c = charge_s[w]
        to = sector + c
        index[w] = jnp.where((to >= 0) & (to < sectors), c + HALO, 2 * HALO + 1)

    reduce_second(INITIAL)
    scale = reduce_last(INITIAL)[0:1]
    v0[...] = v0[...] * lax.rsqrt(scale + 1e-06)
    slots[0][HALO] = v0[...].astype(BF16)
    start_halo(0)

    def apply_local(k):
        half = size // 2

        @pl.loop(0, 2)
        def _(i):
            some = pl.ds(pl.multiple_of(i * half, half), half)
            first = jnp.dot(blk_v[some, :], slots[k][HALO], preferred_element_type=F32)
            acc[some, :] = first + nt_dot(slots[k][HALO, some, :], blk_v[...])

    def term(k, q, t):
        w = q * here + t
        moved = slots[k][index[w]]
        inner = jnp.dot(lbuf[w], moved, preferred_element_type=F32)
        inner = (inner * pat_s[q, rep, t].astype(F32)).astype(BF16)
        return nt_dot(inner, rbuf[w])

    def env_wait(w):
        pltpu.make_async_remote_copy(
            left.at[0, 0, 0], lbuf.at[w], l_send, l_recv.at[w],
            device_id=(ahead, sec, rep), device_id_type=MESH,
        ).wait_recv()
        pltpu.make_async_remote_copy(
            right.at[0, 0, 0], rbuf.at[w], r_send, r_recv.at[w],
            device_id=(behind, sec, rep), device_id_type=MESH,
        ).wait_recv()

    def apply_rest(k):
        wait_halo(k)

        @pl.loop(0, here)
        def _(t):
            acc[...] += term(k, 0, t) + term(k, 1, t)

    def offer(k, x):
        slots[k][HALO] = x.astype(BF16)
        start_halo(k)

    def dot(a, b):
        return column_sums(a * b)

    def coefficients(means, vu, vw, vv, ww):
        alpha = means[vu : vu + 1]
        rest = means[ww : ww + 1] - 2.0 * alpha * means[vw : vw + 1] + alpha * alpha * means[vv : vv + 1]
        return alpha, jnp.sqrt(jnp.maximum(rest, 0.0) + 1e-06)

    apply_local(0)
    wait_halo(0)

    @pl.loop(0, here)
    def _(t):
        env_wait(t)
        env_wait(here + t)
        acc[...] += term(0, 0, t) + term(0, 1, t)

    e1[...] = mask[...] * acc[...]
    offer(1, e1[...])
    reduce_first(0, [dot(v0[...], e1[...]), dot(e1[...], e1[...]), dot(v0[...], v0[...])])
    apply_local(1)
    reduce_second(0)
    apply_rest(1)

    e2[...] = mask[...] * acc[...]
    offer(2, e2[...])
    alpha0, beta0 = coefficients(reduce_last(0), 0, 0, 2, 1)
    inverse0 = 1.0 / beta0
    v1[...] = (e1[...] - alpha0 * v0[...]) * inverse0
    u1[...] = (e2[...] - alpha0 * e1[...]) * inverse0
    w1[...] = u1[...] - beta0 * v0[...]
    reduce_first(1, [dot(v1[...], u1[...]), dot(v1[...], w1[...]), dot(v1[...], v1[...]), dot(w1[...], w1[...])])
    apply_local(2)
    reduce_second(1)
    apply_rest(2)

    hu1[...] = (mask[...] * acc[...] - alpha0 * e2[...]) * inverse0
    hw1[...] = hu1[...] - beta0 * e1[...]
    offer(3, hw1[...])
    apply_local(3)
    alpha1, beta1 = coefficients(reduce_last(1), 0, 1, 2, 3)
    inverse1 = 1.0 / beta1
    mine[0] = (w1[...] - alpha1 * v1[...]) * inverse1
    mine[1] = (hw1[...] - alpha1 * u1[...]) * inverse1
    mine[2] = mine[1] - beta1 * v1[...]

    def final_copy(i):
        return pltpu.make_async_remote_copy(
            mine.at[i], theirs.at[i], fin_send.at[i], fin_recv.at[i],
            device_id=(seg, sec, other), device_id_type=MESH,
        )

    for i in range(3):
        final_copy(i).start()
    hu1[...] = alpha1 * hu1[...] + beta1 * beta1 * u1[...]
    v2, u2, w2 = mine[0], mine[1], mine[2]
    early = [dot(v2, u2), dot(v2, w2), dot(v2, v2), dot(w2, w2), dot(w2, u2), dot(u2, u2)]
    apply_rest(3)

    mine[3] = (mask[...] * acc[...] - hu1[...]) * inverse1
    h, v2, u2, w2 = mine[3], mine[0], mine[1], mine[2]
    reduce_first(2, early + [dot(w2, h), dot(v2, h), dot(h, h), dot(u2, h)])
    final_copy(3).start()
    reduce_second(2)
    means = reduce_last(2)
    vu, vw, vv, ww, wu, uu, wh, vh, hh, uh = (means[i : i + 1] for i in range(10))
    alpha2, beta2 = coefficients(means, 0, 1, 2, 3)
    square2 = beta2 * beta2
    inverse2 = 1.0 / square2
    alpha3 = (wh - alpha2 * (wu + vh) + alpha2 * alpha2 * vu) * inverse2
    ww3 = (
        hh + alpha2 * alpha2 * uu + square2 * square2 * vv
        - 2.0 * (alpha2 * uh + square2 * vh) + 2.0 * alpha2 * square2 * vu
    ) * inverse2
    vv3 = (ww - 2.0 * alpha2 * vw + alpha2 * alpha2 * vv) * inverse2
    vw3 = alpha3 - vw + alpha2 * vv
    rest = ww3 - 2.0 * alpha3 * vw3 + alpha3 * alpha3 * vv3
    beta3 = jnp.sqrt(jnp.maximum(rest, 0.0) + 1e-06)
    coeffs[...] = jnp.concatenate([alpha0, alpha1, alpha2, alpha3, beta0, beta1, beta2, beta3], axis=1)
    outer = 1.0 / (beta2 * beta3)
    along_v = (alpha3 * alpha2 - square2) * outer
    along_u, along_w = -alpha2 * outer, -alpha3 * outer

    def last_vector(parts):
        return outer * parts[3] + along_u * parts[1] + along_w * parts[2] + along_v * parts[0]

    out[0, rep] = last_vector(mine)
    for i in range(4):
        final_copy(i).wait_recv()
    out[0, other] = last_vector(theirs)

    pltpu.make_async_copy(left, left, l_send).wait()
    pltpu.make_async_copy(right, right, r_send).wait()
    pat_copy.wait_send()
    for i in range(4):
        final_copy(i).wait_send()
    for k in range(ITERS):
        for n, d in enumerate(shifts):
            pltpu.make_async_remote_copy(
                slots[k].at[HALO], slots[k].at[HALO - d],
                halo_send.at[k, n], halo_recv.at[k, n],
                device_id=at_sector(d), device_id_type=MESH,
            ).wait_send()
    for k in range(ROUNDS):
        exchange_wait(red_z, k, nz - 1, z_send)
        exchange_wait(red_y, k, 2 * NY - 1, y_send)


def on_device(nseg, nsec, psi, left, right, block, keep_l, keep_r, pattern, charge):
    here, size = left.shape[1], left.shape[3]
    count = 2 * nsec * size * size
    nz = nsec // NY
    vmem = pl.BlockSpec(memory_space=pltpu.VMEM)
    hbm = pl.BlockSpec(memory_space=pltpu.HBM)
    square = (size, size)
    dma = pltpu.SemaphoreType.DMA
    halo = pltpu.VMEM((2 * HALO + 2, *square), BF16)
    terms = 2 * here
    return pl.pallas_call(
        functools.partial(kernel, nseg, nsec, here, size, count),
        out_shape=(
            jax.ShapeDtypeStruct(psi.shape, F32),
            jax.ShapeDtypeStruct((1, 2 * ITERS), F32),
        ),
        in_specs=[hbm] * 8,
        out_specs=(vmem, vmem),
        scratch_shapes=[
            pltpu.VMEM((terms, *square), BF16),
            pltpu.VMEM((terms, *square), BF16),
            halo, halo, halo, halo,
            pltpu.VMEM(square, F32),
            pltpu.VMEM(square, F32),
            *[pltpu.VMEM(square, F32)] * 8,
            pltpu.VMEM((4, *square), F32),
            pltpu.VMEM((4, *square), F32),
            pltpu.VMEM(square, F32),
            pltpu.VMEM(square, BF16),
            pltpu.VMEM((2, here), jnp.int32),
            pltpu.SMEM((2, 2, here), jnp.int32),
            pltpu.SMEM((1, 2), jnp.int32),
            pltpu.SMEM((1, 2), jnp.int32),
            pltpu.SMEM((terms,), jnp.int32),
            pltpu.SMEM((terms,), jnp.int32),
            pltpu.VMEM((ROUNDS, nz, SUMS, 128), F32),
            pltpu.VMEM((ROUNDS, 2 * NY, SUMS, 128), F32),
            dma((6,)), dma, dma, dma((terms,)), dma((terms,)),
            dma((ITERS, 4)), dma((ITERS, 4)),
            dma((ROUNDS,)), dma((ROUNDS,)),
            dma((ROUNDS,)), dma((ROUNDS,)),
            dma, dma, dma((4,)), dma((4,)),
        ],
        compiler_params=pltpu.CompilerParams(
            collective_id=0, has_side_effects=True, vmem_limit_bytes=60 << 20
        ),
    )(psi, left, right, block, keep_l, keep_r, jnp.transpose(pattern, (0, 2, 1)), charge)


def solution(mesh):
    placed = (
        P("seg", "sec", None, None),
        P("seg", "rep", "sec", None, None),
        P("seg", "rep", "sec", None, None),
        P("seg", "sec", None, None),
        P("seg", "sec"),
        P("seg", "sec"),
        P("seg", "rep", "sec"),
        P(),
    )
    return jax.shard_map(
        functools.partial(on_device, mesh.shape["seg"], mesh.shape["sec"]),
        mesh=mesh,
        in_specs=placed,
        out_specs=(P("seg", "sec", None, None), P("seg", None)),
        check_vma=False,
    )
```

time: 117 us -> 110 us (0.940)
  local copies, waits for them, and re-layouts: 9.36 us -> 2.97 us
    unnamed x17 -> x2, local copies, waits for them, and re-layouts: 9.36 us -> 2.97 us
where the time goes in v2:
time: 110 us; the launch traced here: 108 us
  Pallas kernels  105 us (95%)
  local copies, waits for them, and re-layouts  2.97 us (3%)
    pallas_call x1, Pallas kernels, on_device(): pl.pallas_call(functools.partial(kernel, nseg, nsec, here, size, count),...  105 us
    unnamed x2, local copies, waits for them, and re-layouts  2.97 us

profile of v2, /device:TPU:8, one launch (start us, length us, event | category | flops | bytes accessed | tf_op | source)
XLA Modules:
  0.0 108.5 jit_solution(15164546039494990199)
XLA Ops:
  0.6 104.9 %shard_map.95 = (f32[1,2,256,256]{3,2,1,0:T(8,128)}, f32[1,8]{1,0:T(1,128)}) custom-call(f32[1,2,256,256]{3,2,1,0:T(8,128)} %psi.1, bf16[1,9,2,256,256]{4,3,2,1,0:T(8,128)(2,1)} %left.1, bf16[1,9,2,256,256]{4,3,2,1,0:T(8,128)(2,1)} %right.1, bf16[1,2,256,256]{3,2,1,0:T(8,128)(2,1)} %block.1, s32[1,2]{1,0:T(1,128)} %keep_l.1, s32[1,2]{1,0:T(1,128)} %keep_r.1, ...), custom_call_target="tpu_custom_call" | custom-call | tf_op jit(solution)/shard_map/pallas_call | solution.py:340
  105.5 1.9 %copy.12 = f32[1,2,256,256]{3,2,1,0:T(8,128)} copy(f32[1,2,256,256]{3,2,1,0:T(8,128)} %get-tuple-element.4) | data formatting | bytes 1048576
  107.4 1.1 %copy.13 = f32[1,8]{1,0:T(1,128)} copy(f32[1,8]{1,0:T(1,128)} %get-tuple-element.5) | data formatting | bytes 64

commit v3 on v2

--- a/solution.py
+++ b/solution.py
@@ -210,10 +210,11 @@
 
     def apply_rest(k):
         wait_halo(k)
-
-        @pl.loop(0, here)
-        def _(t):
-            acc[...] += term(k, 0, t) + term(k, 1, t)
+        total = acc[...]
+        for t in range(here):
+            for q in range(2):
+                total = total + term(k, q, t)
+        acc[...] = total
 
     def offer(k, x):
         slots[k][HALO] = x.astype(BF16)

time: 110 us -> 105 us (0.955)
  Pallas kernels: 105 us -> 99.3 us
    pallas_call x1, Pallas kernels: 105 us -> 99.3 us  [on_device(): pl.pallas_call(functools.partial(kernel, nseg, nsec, here, size, count),...]
where the time goes in v3:
time: 105 us; the launch traced here: 103 us
  Pallas kernels  99.3 us (95%)
  local copies, waits for them, and re-layouts  2.97 us (3%)
    pallas_call x1, Pallas kernels, on_device(): pl.pallas_call(functools.partial(kernel, nseg, nsec, here, size, count),...  99.3 us
    unnamed x2, local copies, waits for them, and re-layouts  2.97 us

profile of v3, /device:TPU:8, one launch (start us, length us, event | category | flops | bytes accessed | tf_op | source)
XLA Modules:
  0.0 103.0 jit_solution(989144318262219068)
XLA Ops:
  0.6 99.3 %shard_map.95 = (f32[1,2,256,256]{3,2,1,0:T(8,128)}, f32[1,8]{1,0:T(1,128)}) custom-call(f32[1,2,256,256]{3,2,1,0:T(8,128)} %psi.1, bf16[1,9,2,256,256]{4,3,2,1,0:T(8,128)(2,1)} %left.1, bf16[1,9,2,256,256]{4,3,2,1,0:T(8,128)(2,1)} %right.1, bf16[1,2,256,256]{3,2,1,0:T(8,128)(2,1)} %block.1, s32[1,2]{1,0:T(1,128)} %keep_l.1, s32[1,2]{1,0:T(1,128)} %keep_r.1, ...), custom_call_target="tpu_custom_call" | custom-call | tf_op jit(solution)/shard_map/pallas_call | solution.py:341
  100.0 1.9 %copy.12 = f32[1,2,256,256]{3,2,1,0:T(8,128)} copy(f32[1,2,256,256]{3,2,1,0:T(8,128)} %get-tuple-element.4) | data formatting | bytes 1048576
  101.8 1.1 %copy.13 = f32[1,8]{1,0:T(1,128)} copy(f32[1,8]{1,0:T(1,128)} %get-tuple-element.5) | data formatting | bytes 64

commit v4 on v3

--- a/solution.py
+++ b/solution.py
@@ -54,7 +54,8 @@
         s = (sector + sectors + shift) % sectors
         return (seg, s // 2, s % 2)
 
-    shifts = (-1, 1, -2, 2)
+    sign = 2 * rep - 1
+    shifts = (sign, 2 * sign, -2 * sign, -sign)
     z_peers = [(seg, ((z + i) % nz) * NY + y, rep) for i in outward(nz)]
     mine_y = 2 * y + rep
     y_peers = []
@@ -131,10 +132,13 @@
             total = total + buf[k, i]
         return total
 
+    lanes = lax.broadcasted_iota(jnp.int32, (SUMS, 128), 1)
+    diagonal = lanes == lax.broadcasted_iota(jnp.int32, (SUMS, 128), 0)
+
     def reduce_first(k, rows):
-        red_z[k, z] = jnp.zeros_like(red_z[k, 0])
-        for i, row in enumerate(rows):
-            red_z[k, z, pl.ds(i, 1), :] = row
+        rows = rows + [jnp.zeros((SUMS - len(rows), 128), F32)]
+        sums = jnp.sum(jnp.concatenate(rows, axis=0), axis=1, keepdims=True)
+        red_z[k, z] = jnp.sum(jnp.where(diagonal, sums, 0.0), axis=0, keepdims=True)
         exchange_start(red_z, k, z, z_peers, z_send, z_recv)
 
     def reduce_second(k):
@@ -144,8 +148,8 @@
 
     def reduce_last(k):
         exchange_wait(red_y, k, 2 * NY - 1, y_recv)
-        total = jnp.sum(total_of(red_y, k, 2 * NY), axis=1, keepdims=True)
-        return total * (1.0 / count)
+        total = jnp.where(diagonal, total_of(red_y, k, 2 * NY), 0.0)
+        return jnp.sum(total, axis=1, keepdims=True) * (1.0 / count)
 
     pat_copy = pltpu.make_async_remote_copy(
         pattern.at[0], pat_v, pat_send, pat_recv, device_id=(seg, sec, other), device_id_type=MESH
@@ -332,6 +336,7 @@
     here, size = left.shape[1], left.shape[3]
     count = 2 * nsec * size * size
     nz = nsec // NY
+    pin = lambda x: pltpu.with_memory_space_constraint(x, pltpu.HBM)
     vmem = pl.BlockSpec(memory_space=pltpu.VMEM)
     hbm = pl.BlockSpec(memory_space=pltpu.HBM)
     square = (size, size)
@@ -363,8 +368,8 @@
             pltpu.SMEM((1, 2), jnp.int32),
             pltpu.SMEM((terms,), jnp.int32),
             pltpu.SMEM((terms,), jnp.int32),
-            pltpu.VMEM((ROUNDS, nz, SUMS, 128), F32),
-            pltpu.VMEM((ROUNDS, 2 * NY, SUMS, 128), F32),
+            pltpu.VMEM((ROUNDS, nz, 1, 128), F32),
+            pltpu.VMEM((ROUNDS, 2 * NY, 1, 128), F32),
             dma((6,)), dma, dma, dma((terms,)), dma((terms,)),
             dma((ITERS, 4)), dma((ITERS, 4)),
             dma((ROUNDS,)), dma((ROUNDS,)),
@@ -372,9 +377,9 @@
             dma, dma, dma((4,)), dma((4,)),
         ],
         compiler_params=pltpu.CompilerParams(
-            collective_id=0, has_side_effects=True, vmem_limit_bytes=60 << 20
+            collective_id=0, has_side_effects=True, vmem_limit_bytes=48 << 20
         ),
-    )(psi, left, right, block, keep_l, keep_r, jnp.transpose(pattern, (0, 2, 1)), charge)
+    )(*map(pin, (psi, left, right, block, keep_l, keep_r, jnp.transpose(pattern, (0, 2, 1)), charge)))
 
 
 def solution(mesh):

time: 105 us -> 100 us (0.952)
  Pallas kernels: 99.3 us -> 96.8 us
  local copies, waits for them, and re-layouts: 2.97 us -> 1.31 us
    pallas_call x1, Pallas kernels: 99.3 us -> 96.8 us  [on_device(): pl.pallas_call(functools.partial(kernel, nseg, nsec, here, size, count),...]
    unnamed x2, local copies, waits for them, and re-layouts: 2.97 us -> 1.31 us
where the time goes in v4:
time: 100 us; the launch traced here: 98.8 us
  Pallas kernels  96.8 us (97%)
  local copies, waits for them, and re-layouts  1.31 us (1%)
    pallas_call x1, Pallas kernels, on_device(): pl.pallas_call(functools.partial(kernel, nseg, nsec, here, size, count),...  96.8 us

profile of v4, /device:TPU:8, one launch (start us, length us, event | category | flops | bytes accessed | tf_op | source)
XLA Modules:
  0.0 98.8 jit_solution(2569393764775860324)
XLA Ops:
  0.6 96.8 %shard_map.95 = (f32[1,2,256,256]{3,2,1,0:T(8,128)S(1)}, f32[1,8]{1,0:T(1,128)S(1)}) custom-call(f32[1,2,256,256]{3,2,1,0:T(8,128)} %psi.1, bf16[1,9,2,256,256]{4,3,2,1,0:T(8,128)(2,1)} %left.1, bf16[1,9,2,256,256]{4,3,2,1,0:T(8,128)(2,1)} %right.1, bf16[1,2,256,256]{3,2,1,0:T(8,128)(2,1)} %block.1, s32[1,2]{1,0:T(1,128)} %keep_l.1, s32[1,2]{1,0:T(1,128)} %keep_r.1, ...), custom_call_target="tpu_custom_call" | custom-call | tf_op jit(solution)/shard_map/pallas_call | solution.py:346
  97.5 0.8 copy.12
  98.3 0.5 copy.13

commit v5 on v4

--- a/solution.py
+++ b/solution.py
@@ -38,7 +38,7 @@
     out, coeffs,
     lbuf, rbuf, vs0, vs1, vs2, vs3, acc, mask, v0, e1, e2, v1, u1, w1, hu1, hw1, mine, theirs,
     psi_v, blk_v, pat_v, pat_s, kl_s, kr_s, charge_s, index, red_z, red_y,
-    load, l_send, r_send, l_recv, r_recv, halo_send, halo_recv,
+    near_sem, far_sem, load, l_send, r_send, l_recv, r_recv, halo_send, halo_recv,
     z_send, z_recv, y_send, y_recv, pat_send, pat_recv, fin_send, fin_recv,
 ):
     slots = (vs0, vs1, vs2, vs3)
@@ -63,8 +63,13 @@
         p = (mine_y + i) % (2 * NY)
         y_peers.append((seg, z * NY + p // 2, p % 2))
 
+    def at_yz(dy, dz, r):
+        return (seg, ((z + nz + dz) % nz) * NY + (y + NY + dy) % NY, r)
+
     partners = [(a, sec, jnp.int32(r)) for a in (ahead, behind) for r in range(2)]
-    partners += [at_sector(d) for d in shifts] + z_peers + y_peers
+    partners += [at_yz(0, d, rep) for d in (-1, 1)]
+    partners += [at_yz(d, 0, jnp.int32(r)) for d in (-1, 1) for r in range(2)]
+    partners += [(seg, sec, other)]
     barrier = pltpu.get_barrier_semaphore()
     for p in partners:
         pl.semaphore_signal(barrier, inc=1, device_id=p, device_id_type=MESH)
@@ -83,21 +88,21 @@
         w = rep * here + t
         return pltpu.make_async_remote_copy(
             left.at[0, t, r], lbuf.at[w], l_send, l_recv.at[w],
-            device_id=(ahead, sec, jnp.int32(r)), device_id_type=MESH,
+            device_id=(ahead, sec, r), device_id_type=MESH,
         )
 
     def right_copy(t, r):
         w = rep * here + t
         return pltpu.make_async_remote_copy(
             right.at[0, t, r], rbuf.at[w], r_send, r_recv.at[w],
-            device_id=(behind, sec, jnp.int32(r)), device_id_type=MESH,
+            device_id=(behind, sec, r), device_id_type=MESH,
         )
 
-    @pl.loop(0, here)
-    def _(t):
-        for r in range(2):
-            left_copy(t, r).start()
-            right_copy(t, r).start()
+    for i in range(2):
+        @pl.loop(0, here)
+        def _(t):
+            left_copy(t, (sec + i) % 2).start()
+            right_copy(t, (sec + i) % 2).start()
 
     def start_halo(k):
         for n, d in enumerate(shifts):
@@ -150,6 +155,15 @@
         exchange_wait(red_y, k, 2 * NY - 1, y_recv)
         total = jnp.where(diagonal, total_of(red_y, k, 2 * NY), 0.0)
         return jnp.sum(total, axis=1, keepdims=True) * (1.0 / count)
+
+    near = [at_yz(0, d, rep) for d in (-1, 1)] + [at_yz(d, 0, rep) for d in (-1, 1)]
+    for p in near:
+        pl.semaphore_signal(near_sem, inc=1, device_id=p, device_id_type=MESH)
+    pl.semaphore_wait(near_sem, len(near))
+    far = [at_yz(0, d, rep) for d in (-2, 2)]
+    for p in far:
+        pl.semaphore_signal(far_sem, inc=1, device_id=p, device_id_type=MESH)
+    pl.semaphore_wait(far_sem, len(far))
 
     pat_copy = pltpu.make_async_remote_copy(
         pattern.at[0], pat_v, pat_send, pat_recv, device_id=(seg, sec, other), device_id_type=MESH
@@ -370,6 +384,7 @@
             pltpu.SMEM((terms,), jnp.int32),
             pltpu.VMEM((ROUNDS, nz, 1, 128), F32),
             pltpu.VMEM((ROUNDS, 2 * NY, 1, 128), F32),
+            pltpu.SemaphoreType.REGULAR, pltpu.SemaphoreType.REGULAR,
             dma((6,)), dma, dma, dma((terms,)), dma((terms,)),
             dma((ITERS, 4)), dma((ITERS, 4)),
             dma((ROUNDS,)), dma((ROUNDS,)),

time: 100 us -> 98.3 us (0.983)
  Pallas kernels: 96.8 us -> 94.8 us
    pallas_call x1, Pallas kernels: 96.8 us -> 94.8 us  [on_device(): pl.pallas_call(functools.partial(kernel, nseg, nsec, here, size, count),...]
where the time goes in v5:
time: 98.3 us; the launch traced here: 96.7 us
  Pallas kernels  94.8 us (96%)
  local copies, waits for them, and re-layouts  1.31 us (1%)
    pallas_call x1, Pallas kernels, on_device(): pl.pallas_call(functools.partial(kernel, nseg, nsec, here, size, count),...  94.8 us

profile of v5, /device:TPU:8, one launch (start us, length us, event | category | flops | bytes accessed | tf_op | source)
XLA Modules:
  0.0 96.7 jit_solution(16700043274710460059)
XLA Ops:
  0.6 94.8 %shard_map.95 = (f32[1,2,256,256]{3,2,1,0:T(8,128)S(1)}, f32[1,8]{1,0:T(1,128)S(1)}) custom-call(f32[1,2,256,256]{3,2,1,0:T(8,128)} %psi.1, bf16[1,9,2,256,256]{4,3,2,1,0:T(8,128)(2,1)} %left.1, bf16[1,9,2,256,256]{4,3,2,1,0:T(8,128)(2,1)} %right.1, bf16[1,2,256,256]{3,2,1,0:T(8,128)(2,1)} %block.1, s32[1,2]{1,0:T(1,128)} %keep_l.1, s32[1,2]{1,0:T(1,128)} %keep_r.1, ...), custom_call_target="tpu_custom_call" | custom-call | tf_op jit(solution)/shard_map/pallas_call | solution.py:360
  95.4 0.8 copy.12
  96.2 0.5 copy.13

commit v6 on v5

--- a/solution.py
+++ b/solution.py
@@ -143,17 +143,17 @@
     def reduce_first(k, rows):
         rows = rows + [jnp.zeros((SUMS - len(rows), 128), F32)]
         sums = jnp.sum(jnp.concatenate(rows, axis=0), axis=1, keepdims=True)
-        red_z[k, z] = jnp.sum(jnp.where(diagonal, sums, 0.0), axis=0, keepdims=True)
+        red_y[k, mine_y] = jnp.sum(jnp.where(diagonal, sums, 0.0), axis=0, keepdims=True)
+        exchange_start(red_y, k, mine_y, y_peers, y_send, y_recv)
+
+    def reduce_second(k):
+        exchange_wait(red_y, k, 2 * NY - 1, y_recv)
+        red_z[k, z] = total_of(red_y, k, 2 * NY)
         exchange_start(red_z, k, z, z_peers, z_send, z_recv)
 
-    def reduce_second(k):
+    def reduce_last(k):
         exchange_wait(red_z, k, nz - 1, z_recv)
-        red_y[k, mine_y] = total_of(red_z, k, nz)
-        exchange_start(red_y, k, mine_y, y_peers, y_send, y_recv)
-
-    def reduce_last(k):
-        exchange_wait(red_y, k, 2 * NY - 1, y_recv)
-        total = jnp.where(diagonal, total_of(red_y, k, 2 * NY), 0.0)
+        total = jnp.where(diagonal, total_of(red_z, k, nz), 0.0)
         return jnp.sum(total, axis=1, keepdims=True) * (1.0 / count)
 
     near = [at_yz(0, d, rep) for d in (-1, 1)] + [at_yz(d, 0, rep) for d in (-1, 1)]
@@ -232,7 +232,7 @@
         for t in range(here):
             for q in range(2):
                 total = total + term(k, q, t)
-        acc[...] = total
+        return total
 
     def offer(k, x):
         slots[k][HALO] = x.astype(BF16)
@@ -255,28 +255,29 @@
         env_wait(here + t)
         acc[...] += term(0, 0, t) + term(0, 1, t)
 
+    offer(1, mask[...] * acc[...])
     e1[...] = mask[...] * acc[...]
-    offer(1, e1[...])
     reduce_first(0, [dot(v0[...], e1[...]), dot(e1[...], e1[...]), dot(v0[...], v0[...])])
     apply_local(1)
+    total = apply_rest(1)
+
+    offer(2, mask[...] * total)
+    e2[...] = mask[...] * total
     reduce_second(0)
-    apply_rest(1)
-
-    e2[...] = mask[...] * acc[...]
-    offer(2, e2[...])
+    apply_local(2)
     alpha0, beta0 = coefficients(reduce_last(0), 0, 0, 2, 1)
     inverse0 = 1.0 / beta0
     v1[...] = (e1[...] - alpha0 * v0[...]) * inverse0
     u1[...] = (e2[...] - alpha0 * e1[...]) * inverse0
     w1[...] = u1[...] - beta0 * v0[...]
     reduce_first(1, [dot(v1[...], u1[...]), dot(v1[...], w1[...]), dot(v1[...], v1[...]), dot(w1[...], w1[...])])
-    apply_local(2)
+    total = apply_rest(2)
+
+    image = (mask[...] * total - alpha0 * e2[...]) * inverse0
+    offer(3, image - beta0 * e1[...])
+    hu1[...] = image
+    hw1[...] = image - beta0 * e1[...]
     reduce_second(1)
-    apply_rest(2)
-
-    hu1[...] = (mask[...] * acc[...] - alpha0 * e2[...]) * inverse0
-    hw1[...] = hu1[...] - beta0 * e1[...]
-    offer(3, hw1[...])
     apply_local(3)
     alpha1, beta1 = coefficients(reduce_last(1), 0, 1, 2, 3)
     inverse1 = 1.0 / beta1
@@ -295,9 +296,9 @@
     hu1[...] = alpha1 * hu1[...] + beta1 * beta1 * u1[...]
     v2, u2, w2 = mine[0], mine[1], mine[2]
     early = [dot(v2, u2), dot(v2, w2), dot(v2, v2), dot(w2, w2), dot(w2, u2), dot(u2, u2)]
-    apply_rest(3)
-
-    mine[3] = (mask[...] * acc[...] - hu1[...]) * inverse1
+    total = apply_rest(3)
+
+    mine[3] = (mask[...] * total - hu1[...]) * inverse1
     h, v2, u2, w2 = mine[3], mine[0], mine[1], mine[2]
     reduce_first(2, early + [dot(w2, h), dot(v2, h), dot(h, h), dot(u2, h)])
     final_copy(3).start()

time: 98.3 us -> 97.2 us (0.989)
  no operation moved by 1% of the time
where the time goes in v6:
time: 97.2 us; the launch traced here: 96.5 us
  Pallas kernels  94.5 us (97%)
  local copies, waits for them, and re-layouts  1.31 us (1%)
    pallas_call x1, Pallas kernels, on_device(): pl.pallas_call(functools.partial(kernel, nseg, nsec, here, size, count),...  94.5 us

profile of v6, /device:TPU:8, one launch (start us, length us, event | category | flops | bytes accessed | tf_op | source)
XLA Modules:
  0.0 96.5 jit_solution(3943387735307607733)
XLA Ops:
  0.6 94.5 %shard_map.95 = (f32[1,2,256,256]{3,2,1,0:T(8,128)S(1)}, f32[1,8]{1,0:T(1,128)S(1)}) custom-call(f32[1,2,256,256]{3,2,1,0:T(8,128)} %psi.1, bf16[1,9,2,256,256]{4,3,2,1,0:T(8,128)(2,1)} %left.1, bf16[1,9,2,256,256]{4,3,2,1,0:T(8,128)(2,1)} %right.1, bf16[1,2,256,256]{3,2,1,0:T(8,128)(2,1)} %block.1, s32[1,2]{1,0:T(1,128)} %keep_l.1, s32[1,2]{1,0:T(1,128)} %keep_r.1, ...), custom_call_target="tpu_custom_call" | custom-call | tf_op jit(solution)/shard_map/pallas_call | solution.py:361
  95.2 0.8 copy.12
  96.0 0.5 copy.13

commit v7 on v6

--- a/solution.py
+++ b/solution.py
@@ -246,6 +246,18 @@
         rest = means[ww : ww + 1] - 2.0 * alpha * means[vw : vw + 1] + alpha * alpha * means[vv : vv + 1]
         return alpha, jnp.sqrt(jnp.maximum(rest, 0.0) + 1e-06)
 
+    def following(alpha, square, vu, vw, vv, ww, wu, uu, wh, vh, hh, uh):
+        inverse = 1.0 / square
+        alpha_next = (wh - alpha * (wu + vh) + alpha * alpha * vu) * inverse
+        ww_next = (
+            hh + alpha * alpha * uu + square * square * vv
+            - 2.0 * (alpha * uh + square * vh) + 2.0 * alpha * square * vu
+        ) * inverse
+        vv_next = (ww - 2.0 * alpha * vw + alpha * alpha * vv) * inverse
+        vw_next = alpha_next - vw + alpha * vv
+        rest = ww_next - 2.0 * alpha_next * vw_next + alpha_next * alpha_next * vv_next
+        return alpha_next, jnp.sqrt(jnp.maximum(rest, 0.0) + 1e-06)
+
     apply_local(0)
     wait_halo(0)
 
@@ -264,14 +276,12 @@
     offer(2, mask[...] * total)
     e2[...] = mask[...] * total
     reduce_second(0)
+    reduce_first(1, [dot(e1[...], e2[...]), dot(v0[...], e2[...]), dot(e2[...], e2[...])])
     apply_local(2)
-    alpha0, beta0 = coefficients(reduce_last(0), 0, 0, 2, 1)
+    total = apply_rest(2)
+    means0 = reduce_last(0)
+    alpha0, beta0 = coefficients(means0, 0, 0, 2, 1)
     inverse0 = 1.0 / beta0
-    v1[...] = (e1[...] - alpha0 * v0[...]) * inverse0
-    u1[...] = (e2[...] - alpha0 * e1[...]) * inverse0
-    w1[...] = u1[...] - beta0 * v0[...]
-    reduce_first(1, [dot(v1[...], u1[...]), dot(v1[...], w1[...]), dot(v1[...], v1[...]), dot(w1[...], w1[...])])
-    total = apply_rest(2)
 
     image = (mask[...] * total - alpha0 * e2[...]) * inverse0
     offer(3, image - beta0 * e1[...])
@@ -279,7 +289,13 @@
     hw1[...] = image - beta0 * e1[...]
     reduce_second(1)
     apply_local(3)
-    alpha1, beta1 = coefficients(reduce_last(1), 0, 1, 2, 3)
+    v1[...] = (e1[...] - alpha0 * v0[...]) * inverse0
+    u1[...] = (e2[...] - alpha0 * e1[...]) * inverse0
+    w1[...] = u1[...] - beta0 * v0[...]
+    means1 = reduce_last(1)
+    vu0, uu0, vv0 = (means0[i : i + 1] for i in range(3))
+    uh0, vh0, hh0 = (means1[i : i + 1] for i in range(3))
+    alpha1, beta1 = following(alpha0, beta0 * beta0, vu0, vu0, vv0, uu0, uu0, uu0, uh0, vh0, hh0, uh0)
     inverse1 = 1.0 / beta1
     mine[0] = (w1[...] - alpha1 * v1[...]) * inverse1
     mine[1] = (hw1[...] - alpha1 * u1[...]) * inverse1
@@ -303,38 +319,9 @@
     reduce_first(2, early + [dot(w2, h), dot(v2, h), dot(h, h), dot(u2, h)])
     final_copy(3).start()
     reduce_second(2)
-    means = reduce_last(2)
-    vu, vw, vv, ww, wu, uu, wh, vh, hh, uh = (means[i : i + 1] for i in range(10))
-    alpha2, beta2 = coefficients(means, 0, 1, 2, 3)
-    square2 = beta2 * beta2
-    inverse2 = 1.0 / square2
-    alpha3 = (wh - alpha2 * (wu + vh) + alpha2 * alpha2 * vu) * inverse2
-    ww3 = (
-        hh + alpha2 * alpha2 * uu + square2 * square2 * vv
-        - 2.0 * (alpha2 * uh + square2 * vh) + 2.0 * alpha2 * square2 * vu
-    ) * inverse2
-    vv3 = (ww - 2.0 * alpha2 * vw + alpha2 * alpha2 * vv) * inverse2
-    vw3 = alpha3 - vw + alpha2 * vv
-    rest = ww3 - 2.0 * alpha3 * vw3 + alpha3 * alpha3 * vv3
-    beta3 = jnp.sqrt(jnp.maximum(rest, 0.0) + 1e-06)
-    coeffs[...] = jnp.concatenate([alpha0, alpha1, alpha2, alpha3, beta0, beta1, beta2, beta3], axis=1)
-    outer = 1.0 / (beta2 * beta3)
-    along_v = (alpha3 * alpha2 - square2) * outer
-    along_u, along_w = -alpha2 * outer, -alpha3 * outer
-
-    def last_vector(parts):
-        return outer * parts[3] + along_u * parts[1] + along_w * parts[2] + along_v * parts[0]
-
-    out[0, rep] = last_vector(mine)
-    for i in range(4):
-        final_copy(i).wait_recv()
-    out[0, other] = last_vector(theirs)
-
     pltpu.make_async_copy(left, left, l_send).wait()
     pltpu.make_async_copy(right, right, r_send).wait()
     pat_copy.wait_send()
-    for i in range(4):
-        final_copy(i).wait_send()
     for k in range(ITERS):
         for n, d in enumerate(shifts):
             pltpu.make_async_remote_copy(
@@ -342,9 +329,29 @@
                 halo_send.at[k, n], halo_recv.at[k, n],
                 device_id=at_sector(d), device_id_type=MESH,
             ).wait_send()
-    for k in range(ROUNDS):
+    for k in (0, 1, INITIAL):
         exchange_wait(red_z, k, nz - 1, z_send)
         exchange_wait(red_y, k, 2 * NY - 1, y_send)
+    for i in range(4):
+        final_copy(i).wait()
+    means = reduce_last(2)
+    vu, vw, vv, ww, wu, uu, wh, vh, hh, uh = (means[i : i + 1] for i in range(10))
+    alpha2, beta2 = coefficients(means, 0, 1, 2, 3)
+    square2 = beta2 * beta2
+    alpha3, beta3 = following(alpha2, square2, vu, vw, vv, ww, wu, uu, wh, vh, hh, uh)
+    coeffs[...] = jnp.concatenate([alpha0, alpha1, alpha2, alpha3, beta0, beta1, beta2, beta3], axis=1)
+    outer = 1.0 / (beta2 * beta3)
+    along_v = (alpha3 * alpha2 - square2) * outer
+    along_u, along_w = -alpha2 * outer, -alpha3 * outer
+
+    def last_vector(parts):
+        return outer * parts[3] + along_u * parts[1] + along_w * parts[2] + along_v * parts[0]
+
+    out[0, rep] = last_vector(mine)
+    out[0, other] = last_vector(theirs)
+
+    exchange_wait(red_z, 2, nz - 1, z_send)
+    exchange_wait(red_y, 2, 2 * NY - 1, y_send)
 
 
 def on_device(nseg, nsec, psi, left, right, block, keep_l, keep_r, pattern, charge):

time: 97.2 us -> 96.3 us (level)
  no operation moved by 1% of the time
where the time goes in v7:
time: 96.3 us; the launch traced here: 95.5 us
  Pallas kernels  93.6 us (97%)
  local copies, waits for them, and re-layouts  1.31 us (1%)
    pallas_call x1, Pallas kernels, on_device(): pl.pallas_call(functools.partial(kernel, nseg, nsec, here, size, count),...  93.6 us

profile of v7, /device:TPU:8, one launch (start us, length us, event | category | flops | bytes accessed | tf_op | source)
XLA Modules:
  0.0 95.5 jit_solution(4854114009444154501)
XLA Ops:
  0.6 93.6 %shard_map.95 = (f32[1,2,256,256]{3,2,1,0:T(8,128)S(1)}, f32[1,8]{1,0:T(1,128)S(1)}) custom-call(f32[1,2,256,256]{3,2,1,0:T(8,128)} %psi.1, bf16[1,9,2,256,256]{4,3,2,1,0:T(8,128)(2,1)} %left.1, bf16[1,9,2,256,256]{4,3,2,1,0:T(8,128)(2,1)} %right.1, bf16[1,2,256,256]{3,2,1,0:T(8,128)(2,1)} %block.1, s32[1,2]{1,0:T(1,128)} %keep_l.1, s32[1,2]{1,0:T(1,128)} %keep_r.1, ...), custom_call_target="tpu_custom_call" | custom-call | tf_op jit(solution)/shard_map/pallas_call | solution.py:368
  94.2 0.8 copy.12
  95.0 0.5 copy.13

commit v8 on v7

--- a/solution.py
+++ b/solution.py
@@ -307,8 +307,6 @@
             device_id=(seg, sec, other), device_id_type=MESH,
         )
 
-    for i in range(3):
-        final_copy(i).start()
     hu1[...] = alpha1 * hu1[...] + beta1 * beta1 * u1[...]
     v2, u2, w2 = mine[0], mine[1], mine[2]
     early = [dot(v2, u2), dot(v2, w2), dot(v2, v2), dot(w2, w2), dot(w2, u2), dot(u2, u2)]
@@ -317,7 +315,8 @@
     mine[3] = (mask[...] * total - hu1[...]) * inverse1
     h, v2, u2, w2 = mine[3], mine[0], mine[1], mine[2]
     reduce_first(2, early + [dot(w2, h), dot(v2, h), dot(h, h), dot(u2, h)])
-    final_copy(3).start()
+    for i in range(4):
+        final_copy(i).start()
     reduce_second(2)
     pltpu.make_async_copy(left, left, l_send).wait()
     pltpu.make_async_copy(right, right, r_send).wait()

time: 96.3 us -> 96.3 us (level)
  no operation moved by 1% of the time
where the time goes in v8:
time: 96.3 us; the launch traced here: 95.5 us
  Pallas kernels  93.6 us (97%)
  local copies, waits for them, and re-layouts  1.31 us (1%)
    pallas_call x1, Pallas kernels, on_device(): pl.pallas_call(functools.partial(kernel, nseg, nsec, here, size, count),...  93.6 us

profile of v8, /device:TPU:8, one launch (start us, length us, event | category | flops | bytes accessed | tf_op | source)
XLA Modules:
  0.0 95.5 jit_solution(9568509165344451179)
XLA Ops:
  0.6 93.6 %shard_map.95 = (f32[1,2,256,256]{3,2,1,0:T(8,128)S(1)}, f32[1,8]{1,0:T(1,128)S(1)}) custom-call(f32[1,2,256,256]{3,2,1,0:T(8,128)} %psi.1, bf16[1,9,2,256,256]{4,3,2,1,0:T(8,128)(2,1)} %left.1, bf16[1,9,2,256,256]{4,3,2,1,0:T(8,128)(2,1)} %right.1, bf16[1,2,256,256]{3,2,1,0:T(8,128)(2,1)} %block.1, s32[1,2]{1,0:T(1,128)} %keep_l.1, s32[1,2]{1,0:T(1,128)} %keep_r.1, ...), custom_call_target="tpu_custom_call" | custom-call | tf_op jit(solution)/shard_map/pallas_call | solution.py:367
  94.2 0.8 copy.12
  95.0 0.5 copy.13

commit v9 on v8

--- a/solution.py
+++ b/solution.py
@@ -315,9 +315,9 @@
     mine[3] = (mask[...] * total - hu1[...]) * inverse1
     h, v2, u2, w2 = mine[3], mine[0], mine[1], mine[2]
     reduce_first(2, early + [dot(w2, h), dot(v2, h), dot(h, h), dot(u2, h)])
+    reduce_second(2)
     for i in range(4):
         final_copy(i).start()
-    reduce_second(2)
     pltpu.make_async_copy(left, left, l_send).wait()
     pltpu.make_async_copy(right, right, r_send).wait()
     pat_copy.wait_send()

time: 96.3 us -> 96.3 us (level)
  no operation moved by 1% of the time
where the time goes in v9:
time: 96.3 us; the launch traced here: 95.5 us
  Pallas kernels  93.6 us (97%)
  local copies, waits for them, and re-layouts  1.31 us (1%)
    pallas_call x1, Pallas kernels, on_device(): pl.pallas_call(functools.partial(kernel, nseg, nsec, here, size, count),...  93.6 us

profile of v9, /device:TPU:8, one launch (start us, length us, event | category | flops | bytes accessed | tf_op | source)
XLA Modules:
  0.0 95.5 jit_solution(15399832692005056377)
XLA Ops:
  0.6 93.6 %shard_map.95 = (f32[1,2,256,256]{3,2,1,0:T(8,128)S(1)}, f32[1,8]{1,0:T(1,128)S(1)}) custom-call(f32[1,2,256,256]{3,2,1,0:T(8,128)} %psi.1, bf16[1,9,2,256,256]{4,3,2,1,0:T(8,128)(2,1)} %left.1, bf16[1,9,2,256,256]{4,3,2,1,0:T(8,128)(2,1)} %right.1, bf16[1,2,256,256]{3,2,1,0:T(8,128)(2,1)} %block.1, s32[1,2]{1,0:T(1,128)} %keep_l.1, s32[1,2]{1,0:T(1,128)} %keep_r.1, ...), custom_call_target="tpu_custom_call" | custom-call | tf_op jit(solution)/shard_map/pallas_call | solution.py:367
  94.2 0.8 copy.12
  95.0 0.5 copy.13
